TPU v7x, 32 devices: a whole 2x2x4 slice. The times are simulated.
32 devices in a mesh: blk: 8 (over z, x), tile: 4 (over y, core).
Axes of the slice: x: 2, y: 2, z: 4, core: 2. Of those that a mesh axis runs over, the one named last changes fastest.
Arguments:
- stream_in: bfloat16 [32, 16, 16, 2240], P('tile', 'blk'), may hold values from -6 to 6
- queries: bfloat16 [32, 16, 16, 2240], P('tile', 'blk'), may hold values from -12 to 12
- key_rows: bfloat16 [32, 16, 16, 2240], P('tile', 'blk'), may hold values from -12 to 12
- value_rows: bfloat16 [32, 16, 16, 2240], P('tile', 'blk'), may hold values from -12 to 12
- w_output: bfloat16 [2240, 2240], P('tile'), may hold values from -0.125 to 0.125
- w_inner: bfloat16 [2240, 2, 4096], P(None, None, 'tile'), may hold values from -0.125 to 0.125
- w_down: bfloat16 [4096, 2240], P('tile'), may hold values from -0.09375 to 0.09375
- spatial_taps: float32 [3, 3, 2, 4096], P(None, None, None, 'tile'), may hold values from -2 to 2
- temporal_taps: float32 [3, 2, 4096], P(None, None, 'tile'), may hold values from -3.5 to 3.5
Outputs:
- layer_out: bfloat16 [32, 16, 16, 2240], P('tile', 'blk')
All inputs are finite; a program needn't handle non-finite values.
Results may differ from a plain program's by a relative error of at most 0.009.
Values may be sent and summed in bfloat16 or wider, within the bound.
A program may use at most 128 MiB of HBM per device.

v0:
```python
import jax
import jax.numpy as jnp
from jax import lax
from jax.sharding import PartitionSpec as P

HEADS = 20
HEAD_DIM = 112
TAPS = 3
EPS = 1e-06


def from_partner(value, axis, stride):
    mask = 2**stride
    pairs = [(source, source ^ mask) for source in range(lax.axis_size(axis))]
    return lax.ppermute(value, axis, pairs)


def carried_in(x, axis, combine, identity):
    peers, position = (lax.axis_size(axis), lax.axis_index(axis))
    everything = jax.tree.map(lambda part: lax.all_gather(part, axis), x)
    start = jax.tree.map(
        lambda part, zero: jnp.broadcast_to(jnp.asarray(zero, part.dtype), part.shape), x, identity
    )

    def step(k, before):
        reached = k < position
        new = combine(before, jax.tree.map(lambda part: part[k], everything))
        return jax.tree.map(lambda a, b: jnp.where(reached, a, b), new, before)

    return lax.fori_loop(0, peers, step, start)


def shifted(x, axis, by):
    peers = lax.axis_size(axis)
    pairs = [(i, i + by) for i in range(peers) if 0 <= i + by < peers]
    return lax.ppermute(x, axis, pairs)


def add_pair(earlier, later):
    return (earlier[0] + later[0], earlier[1] + later[1])


def prefix_state(state_parts):
    partner = from_partner((state_parts[0], state_parts[1]), "blk", 0)
    block_sum = add_pair(state_parts, partner)
    odd_side = (lax.axis_index("blk") % 2).astype(jnp.float32)
    keep_share = 1.0 - 0.5 * odd_side
    zero_state = (jnp.zeros_like(block_sum[0]), jnp.zeros_like(block_sum[1]))
    before = carried_in((block_sum[0] * 0.5, block_sum[1] * 0.5), "blk", add_pair, zero_state)
    return (before[0] + block_sum[0] * keep_share, before[1] + block_sum[1] * keep_share)


def spatial_conv(inner_act, spatial_taps):
    row_count = inner_act.shape[0]
    col_count = inner_act.shape[2]
    padded = jnp.pad(inner_act, ((1, 1), (0, 0), (1, 1), (0, 0), (0, 0)))
    running = jnp.zeros(inner_act.shape, jnp.float32)
    for tap_row in range(3):
        for tap_col in range(3):
            window = padded[tap_row : tap_row + row_count, :, tap_col : tap_col + col_count]
            running = running + window.astype(jnp.float32) * spatial_taps[tap_row, tap_col]
    return running


def on_device(
    stream_in, queries, key_rows, value_rows, w_output, w_inner, w_down, spatial_taps, temporal_taps
):
    row_count, frames, col_count, model_width = queries.shape
    tokens = row_count * frames * col_count
    highest = lax.Precision.HIGHEST
    key_pos = jax.nn.relu(key_rows).reshape(tokens, HEADS, HEAD_DIM)
    value_heads = value_rows.reshape(tokens, HEADS, HEAD_DIM)
    local_kv = jnp.einsum("thd,the->hde", key_pos, value_heads, preferred_element_type=jnp.float32)
    local_kv = local_kv.reshape(model_width, HEAD_DIM)
    local_z = jnp.sum(key_pos.astype(jnp.float32), axis=0).reshape(model_width)
    shares = (
        lax.psum_scatter(local_kv, "tile", scatter_dimension=0, tiled=True),
        lax.psum_scatter(local_z, "tile", scatter_dimension=0, tiled=True),
    )
    share_state = prefix_state(shares)
    state, zsum = (
        lax.all_gather(share_state[0], "tile", axis=0, tiled=True),
        lax.all_gather(share_state[1], "tile", axis=0, tiled=True),
    )
    state = state.reshape(HEADS, HEAD_DIM, HEAD_DIM)
    zsum = zsum.reshape(HEADS, HEAD_DIM)
    query_pos = jax.nn.relu(queries.astype(jnp.float32)).reshape(tokens, HEADS, HEAD_DIM)
    numerator = jnp.einsum("thd,hde->the", query_pos, state, precision=highest)
    denominator = jnp.einsum("thd,hd->th", query_pos, zsum, precision=highest) + EPS
    attended = (numerator / denominator[..., None]).astype(jnp.bfloat16)
    attended = attended.reshape(row_count, frames, col_count, model_width)
    by_feature = lax.all_to_all(attended, "tile", split_axis=3, concat_axis=0, tiled=True)
    portion = by_feature
    product = jnp.dot(
        portion.reshape(-1, portion.shape[3]), w_output, preferred_element_type=jnp.float32
    )
    attn_out = lax.psum_scatter(
        product.reshape(row_count * lax.axis_size("tile"), frames, col_count, model_width),
        "tile",
        scatter_dimension=0,
        tiled=True,
    )
    hidden = (stream_in.astype(jnp.float32) + attn_out).astype(jnp.bfloat16)
    chan_dev = w_inner.shape[2]
    w_flat = w_inner.reshape(model_width, 2 * chan_dev)
    portion = lax.all_gather(hidden, "tile", axis=0, tiled=True)
    product = jnp.dot(portion.reshape(-1, model_width), w_flat, preferred_element_type=jnp.float32)
    activated = jax.nn.silu(product).astype(jnp.bfloat16)
    inner_act = activated.reshape(portion.shape[0], frames, col_count, 2, chan_dev)
    spatial = spatial_conv(inner_act, spatial_taps).astype(jnp.bfloat16)
    earlier_frames = shifted(spatial, "blk", 1)
    extended = jnp.concatenate([earlier_frames, spatial], axis=1)
    temporal_mix = jnp.zeros(spatial.shape, jnp.float32)
    for lag in range(TAPS):
        window = extended[:, TAPS - 1 - lag : TAPS - 1 - lag + frames]
        temporal_mix = temporal_mix + window.astype(jnp.float32) * temporal_taps[lag]
    gated_out = (temporal_mix[..., 0, :] * jax.nn.silu(temporal_mix[..., 1, :])).astype(
        jnp.bfloat16
    )
    portion = gated_out
    product = jnp.dot(portion.reshape(-1, chan_dev), w_down, preferred_element_type=jnp.float32)
    ffn_out = lax.psum_scatter(
        product.reshape(lax.axis_size("tile") * row_count, frames, col_count, model_width).astype(
            jnp.bfloat16
        ),
        "tile",
        scatter_dimension=0,
        tiled=True,
    ).astype(jnp.float32)
    return (hidden.astype(jnp.float32) + ffn_out).astype(jnp.bfloat16)


def solution(mesh):
    in_specs = (
        P("tile", "blk", None, None),
        P("tile", "blk", None, None),
        P("tile", "blk", None, None),
        P("tile", "blk", None, None),
        P("tile", None),
        P(None, None, "tile"),
        P("tile", None),
        P(None, None, None, "tile"),
        P(None, None, "tile"),
    )
    out_specs = P("tile", "blk", None, None)
    return jax.shard_map(
        on_device, mesh=mesh, in_specs=in_specs, out_specs=out_specs, check_vma=False
    )
```

profile of v0, /device:TPU:0, one launch (start us, length us, event | category | flops | bytes accessed | tf_op | source)
XLA Modules:
  0.0 571.9 jit_solution(4636084456415027600)
XLA Ops:
  9.1 4.0 reshape.58
  20.6 28.2 %reduce-scatter.4.cloned.1.call-done = f32[560,112]{1,0:T(8,128)} async-done(((f32[2240,112]{1,0:T(8,128)}), f32[560,112]{1,0:T(8,128)}) %reduce-scatter.4.cloned.1.call-update) | async-done | bytes 250896 | tf_op jit(solution)/shard_map/reduce_scatter | solution.py:77
  50.3 7.2 %collective-permute-done = f32[560,112]{1,0:T(8,128)S(1)} collective-permute-done((f32[560,112]{1,0:T(8,128)}, f32[560,112]{1,0:T(8,128)S(1)}, u32[]{:S(2)}, u32[]{:S(2)}) %collective-permute-start) | collective-permute-done | bytes 250912 | tf_op jit(solution)/shard_map/ppermute | solution.py:15
  62.2 10.2 %all-reduce.3 = f32[2240]{0:T(1024)S(1)} all-reduce(f32[2240]{0:T(1024)S(1)} %convert_reduce_fusion), channel_id=5, replica_groups=mesh['blk'=8,'tile'=4] {'tile'}, use_global_device_ids=true, to_apply=%region_2.3.clone | all-reduce | flops 2240 | bytes 17920
  79.2 4.3 reshape.62
  87.0 36.8 %all-reduce.1 = f32[4480]{0:T(1024)S(1)} all-reduce(f32[4480]{0:T(1024)S(1)} %multiply_dynamic-update-slice_fusion), channel_id=3, replica_groups=mesh['blk'=8,'tile'=4] {'blk'}, use_global_device_ids=true, to_apply=%add.1 | all-reduce | flops 4480 | bytes 35840
  123.9 8.9 %while.16 = (s32[]{:T(128)}, f32[560,112]{1,0:T(8,128)S(1)}, f32[560]{0:T(1024)S(1)}, s32[]{:T(128)}, f32[8,560,112]{2,1,0:T(8,128)}, /*index=5*/f32[8,560]{1,0:T(8,128)S(1)}, s32[]{:T(128)}, s32[]{:T(128)}) while((s32[]{:T(128)}, f32[560,112]{1,0:T(8,128)S(1)}, f32[560]{0:T(1024)S(1)}, s32[]{:T(128)}, f32[8,560,112]{2,1,0:T(8,128)}, ...), condition=%wide.region_4.5_spmd.clone, body=%wide.region_3.4_spmd.clone.sunk | while | flops 189844 | bytes 763955 | solution.py:30
  133.0 10.1 %all-reduce.2 = f32[2240]{0:T(1024)S(1)} all-reduce(f32[2240]{0:T(1024)S(1)} %add_dynamic-update-slice_fusion), channel_id=1, replica_groups=mesh['blk'=8,'tile'=4] {'tile'}, use_global_device_ids=true, to_apply=%add.2 | all-reduce | flops 2240 | bytes 17920
  146.3 9.7 %all_gather.25 = f32[2240,112]{1,0:T(8,128)S(1)} all-gather(f32[560,112]{1,0:T(8,128)S(1)} %multiply_add_fusion.1), channel_id=1, replica_groups=mesh['blk'=8,'tile'=4] {'tile'}, dimensions={0}, use_global_device_ids=true | all-gather | bytes 1254400 | tf_op jit(solution)/shard_map/all_gather | solution.py:82
  159.2 28.0 %reshape.86 = bf16[8,2,16,2240]{2,1,0,3:T(2,128)(2,1)} reshape(bf16[256,20,112]{0,2,1:T(8,128)(2,1)} %fusion.5) | data formatting | bytes 2293760 | tf_op jit(solution)/shard_map/reshape | solution.py:91
  187.2 11.8 %reshape.89 = bf16[4,2,71680]{2,1,0:T(2,128)(2,1)} reshape(bf16[2240,8,2,16]{3,2,1,0:T(2,128)(2,1)} %bitcast.90) | data formatting | bytes 2293760
  198.9 19.8 %all_to_all.15 = bf16[4,2,71680]{2,1,0:T(2,128)(2,1)} all-to-all(bf16[4,2,71680]{2,1,0:T(2,128)(2,1)} %reshape.89), channel_id=1, replica_groups=mesh['blk'=8,'tile'=4] {'tile'}, dimensions={0} | all-to-all | bytes 2293760 | tf_op jit(solution)/shard_map/all_to_all | solution.py:92
  218.8 8.7 %reshape.90 = bf16[2240,8,2,16]{3,2,1,0:T(2,128)(2,1)} reshape(bf16[4,2,71680]{2,1,0:T(2,128)(2,1)} %all_to_all.15) | data formatting | bytes 2293760
  227.5 19.9 %copy.30 = bf16[8,2,16,4,560]{4,2,1,0,3:T(8,128)(2,1)} copy(bf16[8,2,16,4,560]{2,1,0,4,3:T(2,128)(2,1)} %bitcast.91) | data formatting | bytes 2293760 | tf_op jit(solution)/shard_map/all_to_all | solution.py:92
  247.3 7.8 %fusion.3 = f32[32,2,16,2240]{3,2,1,0:T(8,128)} fusion(bf16[32,2,16,560]{3,2,1,0:T(8,128)(2,1)} %bitcast.95, bf16[560,2240]{1,0:T(8,128)(2,1)S(1)} %copy-done), kind=kOutput, calls=%fused_computation.21 | convolution fusion | flops 2569011200 | bytes 12830720 | tf_op jit(solution)/shard_map/dot_general | solution.py:94
  255.2 74.2 %reduce-scatter.6.cloned.1.call-done = f32[8,2,16,2240]{3,2,1,0:T(8,128)} async-done(((f32[32,2,16,2240]{3,2,1,0:T(8,128)}), f32[8,2,16,2240]{3,2,1,0:T(8,128)}) %reduce-scatter.6.cloned.1.call-update) | async-done | bytes 2293776 | tf_op jit(solution)/shard_map/reduce_scatter | solution.py:97
  332.6 11.4 %copy.38 = bf16[280,8,2,1024]{3,1,2,0:T(8,128)(2,1)} copy(bf16[280,8,2,1024]{3,2,1,0:T(2,128)(2,1)} %bitcast.92) | data formatting | bytes 18350080
  344.1 25.9 %all-gather.5.cloned.1.call-done = bf16[32,2,16,2240]{3,2,1,0:T(8,128)(2,1)} async-done(((bf16[8,2,16,2240]{3,2,1,0:T(8,128)(2,1)}), bf16[32,2,16,2240]{3,2,1,0:T(8,128)(2,1)}) %all-gather.5.cloned.1.call-update) | async-done | bytes 4587536 | tf_op jit(solution)/shard_map/all_gather | solution.py:106
  370.0 16.0 %multiply_convert_fusion = bf16[1024,2048]{1,0:T(8,128)(2,1)} fusion(bf16[1024,2240]{1,0:T(8,128)(2,1)} %bitcast.98, bf16[2240,2048]{1,0:T(8,128)(2,1)} %bitcast.93), kind=kOutput, calls=%fused_computation.13 | convolution fusion | flops 9405726720 | bytes 17956864 | tf_op jit(solution)/shard_map/dot_general | solution.py:107
  386.0 7.8 %reshape.67 = bf16[32,2,16,2,1024]{4,3,2,1,0:T(2,128)(2,1)} reshape(bf16[1024,2048]{1,0:T(8,128)(2,1)} %multiply_convert_fusion) | data formatting | bytes 8388608 | tf_op jit(solution)/shard_map/reshape | solution.py:109
  397.3 11.9 %add_convert_fusion = bf16[32,2,16,2,1024]{4,2,1,0,3:T(8,128)(2,1)S(1)} fusion(bf16[32,2,16,2,1024]{4,2,1,0,3:T(8,128)(2,1)S(1)} %copy.31, f32[2,1024]{1,0:T(2,128)S(1)} %get-tuple-element.157, f32[2,1024]{1,0:T(2,128)S(1)} %get-tuple-element.158, f32[2,1024]{1,0:T(2,128)S(1)} %get-tuple-element.151, f32[2,1024]{1,0:T(2,128)S(1)} %get-tuple-element.152, ...), kind=kLoop, calls=%fused_computation.12 | loop fusion | flops 56623104 | bytes 8462336 | tf_op jit(solution)/shard_map/convert_element_type | solution.py:110
  413.2 89.7 %collective-permute-done.2 = bf16[32,2,16,2,1024]{4,2,1,0,3:T(8,128)(2,1)S(1)} collective-permute-done((bf16[32,2,16,2,1024]{4,2,1,0,3:T(8,128)(2,1)S(1)}, bf16[32,2,16,2,1024]{4,2,1,0,3:T(8,128)(2,1)S(1)}, u32[]{:S(2)}, u32[]{:S(2)}) %collective-permute-start.2) | collective-permute-done | bytes 4194336 | tf_op jit(solution)/shard_map/ppermute | solution.py:36
  506.0 7.3 %convolution_convert_fusion = bf16[32,2,16,2240]{3,2,1,0:T(8,128)(2,1)} fusion(bf16[1024,2240]{0,1:T(8,128)(2,1)S(1)} %bitcast.100, f32[32,2,16,2,1024]{4,2,1,0,3:T(8,128)S(1)} %multiply_add_fusion), kind=kOutput, calls=%fused_computation.14 | convolution fusion | flops 4706205696 | bytes 17563648 | tf_op jit(solution)/shard_map/dot_general | solution.py:121
  513.4 49.1 %reduce-scatter.8.cloned.1.call-done = bf16[8,2,16,2240]{3,2,1,0:T(8,128)(2,1)} async-done(((bf16[32,2,16,2240]{3,2,1,0:T(8,128)(2,1)}), bf16[8,2,16,2240]{3,2,1,0:T(8,128)(2,1)}) %reduce-scatter.8.cloned.1.call-update) | async-done | bytes 1146896 | tf_op jit(solution)/shard_map/reduce_scatter | solution.py:122
  (90 shorter events, 56.6 us)
Async XLA Ops:
  6.5 240.8 %copy-start = (bf16[560,2240]{1,0:T(8,128)(2,1)S(1)}, bf16[560,2240]{1,0:T(8,128)(2,1)}, u32[]{:S(2)}) copy-start(bf16[560,2240]{1,0:T(8,128)(2,1)} %param.15) | copy-start | bytes 7526404
  6.5 42.3 %reduce-scatter.4.cloned.1.call-start = ((), (), s32[]{:S(2)}) async-start(), calls=%async_computation.4 | async-start | bytes 1433600 | tf_op jit(solution)/shard_map/reduce_scatter | solution.py:77
  13.1 46.2 %copy-start.7 = (u32[32]{0:T(128)S(1)}, u32[32]{0:T(128)}, u32[]{:S(2)}) copy-start(u32[32]{0:T(128)} %constant.77) | copy-start | bytes 388
  20.6 56.7 %copy-start.8 = (u32[32]{0:T(128)S(1)}, u32[32]{0:T(128)}, u32[]{:S(2)}) copy-start(u32[32]{0:T(128)} %constant.72) | copy-start | bytes 388
  20.6 103.3 %all-gather.7.cloned.1.call-start = ((), (), s32[]{:S(2)}) async-start(), calls=%async_computation.8 | async-start | bytes 2580480 | tf_op jit(solution)/shard_map/all_gather | solution.py:20
  48.9 8.6 %collective-permute-start = (f32[560,112]{1,0:T(8,128)}, f32[560,112]{1,0:T(8,128)S(1)}, u32[]{:S(2)}, u32[]{:S(2)}) collective-permute-start(f32[560,112]{1,0:T(8,128)} %reduce-scatter.4.cloned.1.call-done), channel_id=1, source_target_pairs={{0,4},{4,0},{8,12},{12,8},{16,20},{20,16},{24,28},{28,24},{1,5},{5... | collective-permute-start | bytes 752648 | tf_op jit(solution)/shard_map/ppermute | solution.py:15
  59.3 270.2 %reduce-scatter.6.cloned.1.call-start = ((), (), s32[]{:S(2)}) async-start(), calls=%async_computation.5 | async-start | bytes 11796480 | tf_op jit(solution)/shard_map/reduce_scatter | solution.py:97
  72.4 14.4 %collective-permute-start.1 = (f32[560]{0:T(1024)S(1)}, f32[560]{0:T(1024)S(1)}, u32[]{:S(2)}, u32[]{:S(2)}) collective-permute-start(f32[560]{0:T(1024)S(1)} %dynamic-slice.3), channel_id=1, source_target_pairs={{0,4},{4,0},{8,12},{12,8},{16,20},{20,16},{24,28},{28,24},{1,5},{5... | collective-permute-start | bytes 6728 | tf_op jit(solution)/shard_map/ppermute | solution.py:15
  86.8 59.4 %copy-start.4 = (f32[560,112]{1,0:T(8,128)S(1)}, f32[560,112]{1,0:T(8,128)}, u32[]{:S(2)}) copy-start(f32[560,112]{1,0:T(8,128)} %reduce-scatter.4.cloned.1.call-done) | copy-start | bytes 752644
  143.2 12.8 %copy-start.2 = (f32[256,20,112]{0,2,1:T(8,128)S(1)}, f32[256,20,112]{0,2,1:T(8,128)}, u32[]{:S(2)}) copy-start(f32[256,20,112]{0,2,1:T(8,128)} %copy.27) | copy-start | bytes 6881284
  255.2 74.3 %copy-start.3 = (bf16[8,2,16,2240]{3,2,1,0:T(8,128)(2,1)S(1)}, bf16[8,2,16,2240]{3,2,1,0:T(8,128)(2,1)}, u32[]{:S(2)}) copy-start(bf16[8,2,16,2240]{3,2,1,0:T(8,128)(2,1)} %param.11) | copy-start | bytes 3440644
  255.2 114.8 %all-gather.5.cloned.1.call-start = ((), (), s32[]{:S(2)}) async-start(), calls=%async_computation.6 | async-start | bytes 5898240 | tf_op jit(solution)/shard_map/all_gather | solution.py:106
  332.4 230.1 %reduce-scatter.8.cloned.1.call-start = ((), (), s32[]{:S(2)}) async-start(), calls=%async_computation.7 | async-start | bytes 5898240 | tf_op jit(solution)/shard_map/reduce_scatter | solution.py:122
  332.6 11.4 %copy-start.5 = (f32[3,3,2,1024]{3,2,1,0:T(2,128)S(1)}, f32[3,3,2,1024]{3,2,1,0:T(2,128)}, u32[]{:S(2)}) copy-start(f32[3,3,2,1024]{3,2,1,0:T(2,128)} %param.18) | copy-start | bytes 221188
  397.3 15.8 %copy-start.6 = (f32[3,2,1024]{2,1,0:T(2,128)S(1)}, f32[3,2,1024]{2,1,0:T(2,128)}, u32[]{:S(2)}) copy-start(f32[3,2,1024]{2,1,0:T(2,128)} %param.19) | copy-start | bytes 73732
  397.3 108.7 %slice-start = ((s8[4587520]{0:T(1024)(128)(4,1)}), s8[4194304]{0:T(1024)(128)(4,1)S(1)}, s32[]{:S(2)}) async-start(s8[4587520]{0:T(1024)(128)(4,1)} %bitcast.99), calls=%async_computation.9 | async-start | bytes 8388608
  409.2 93.6 %collective-permute-start.2 = (bf16[32,2,16,2,1024]{4,2,1,0,3:T(8,128)(2,1)S(1)}, bf16[32,2,16,2,1024]{4,2,1,0,3:T(8,128)(2,1)S(1)}, u32[]{:S(2)}, u32[]{:S(2)}) collective-permute-start(bf16[32,2,16,2,1024]{4,2,1,0,3:T(8,128)(2,1)S(1)} %add_convert_fusion), channel_id=1, source_target_pairs={{0,4},{4,8},{8,12},{12,16},{16,20},{20,24},{24,28},{1,5},{5,9},{9,... | collective-permute-start | bytes 12582920 | tf_op jit(solution)/shard_map/ppermute | solution.py:36
  502.8 3.2 slice-start.1
  506.0 59.4 %copy-start.1 = (bf16[560,2240]{1,0:T(8,128)(2,1)S(1)}, bf16[560,2240]{1,0:T(8,128)(2,1)}, u32[]{:S(2)}) copy-start(bf16[560,2240]{1,0:T(8,128)(2,1)} %param.15) | copy-start | bytes 7526404
Sparse Core Ops, SparseCore 0:
  20.7 28.1 reduce-scatter.3
  59.4 51.7 all-gather.6
  255.3 74.0 reduce-scatter.5
  332.5 37.4 all-gather.4
  513.5 48.9 reduce-scatter.7
where the time goes:
time: 574 us; the launch traced here: 572 us
  waiting for transfers between devices  274 us (48%)
  local copies, waits for them, and re-layouts  108 us (19%)
  blocking collectives  86.6 us (15%)
  matrix products  40.7 us (7%)
  other arithmetic  38.5 us (7%)
  between operations  15.2 us (3%)
  starting transfers between devices  7.66 us (1%)
    ppermute x1, waiting for transfers between devices, shifted(): return lax.ppermute(x, axis, pairs)  89.7 us
    reduce_scatter x1, waiting for transfers between devices, on_device(): lax.psum_scatter(product.reshape(row_count * lax.axis_size('tile'), frame...  74.2 us
    unnamed x3, blocking collectives  57.1 us
    reduce_scatter x1, waiting for transfers between devices, on_device(): lax.psum_scatter(product.reshape(lax.axis_size('tile') * row_count, frame...  49.1 us
    unnamed x30, local copies, waits for them, and re-layouts  33.3 us
    reduce_scatter x1, waiting for transfers between devices, on_device(): lax.psum_scatter(local_kv, 'tile', scatter_dimension=0, tiled=True)  28.2 us
    reshape x1, local copies, waits for them, and re-layouts, on_device(): attended = attended.reshape(row_count, frames, col_count, model_width)  28 us
    all_gather x1, waiting for transfers between devices, on_device(): portion = lax.all_gather(hidden, 'tile', axis=0, tiled=True)  25.9 us
  transfers between devices with their start and end apart: 8, of which 6 were waited for; matrix products, arithmetic and copies ran while one was open for 4% of the time, Pallas kernels for 0%

commit v1 on v0

--- a/solution.py
+++ b/solution.py
@@ -7,6 +7,17 @@
 HEAD_DIM = 112
 TAPS = 3
 EPS = 1e-06
+
+
+def _refer_shards(block_here, axis_id):
+    e_next = lax.all_to_all(
+        jnp.stack(jnp.split(block_here, lax.axis_size(axis_id), axis=3), axis=0),
+        axis_name=axis_id,
+        split_axis=0,
+        concat_axis=0,
+    )
+    passed = jnp.concatenate(e_next, axis=0)
+    return passed
 
 
 def from_partner(value, axis, stride):
@@ -89,7 +100,7 @@
     denominator = jnp.einsum("thd,hd->th", query_pos, zsum, precision=highest) + EPS
     attended = (numerator / denominator[..., None]).astype(jnp.bfloat16)
     attended = attended.reshape(row_count, frames, col_count, model_width)
-    by_feature = lax.all_to_all(attended, "tile", split_axis=3, concat_axis=0, tiled=True)
+    by_feature = _refer_shards(attended, "tile")
     portion = by_feature
     product = jnp.dot(
         portion.reshape(-1, portion.shape[3]), w_output, preferred_element_type=jnp.float32

time: 574 us -> 512 us (0.89)
  local copies, waits for them, and re-layouts: 108 us -> 48.3 us
    reshape x1, local copies, waits for them, and re-layouts: 28 us -> 3.66 us  [on_device(): attended = attended.reshape(row_count, frames, col_count, model_width)]
    unnamed x30 -> x28, local copies, waits for them, and re-layouts: 33.3 us -> 12.8 us
    all_to_all x1 -> x0, local copies, waits for them, and re-layouts: 19.9 us -> none  [on_device(): lax.all_to_all(attended, 'tile', split_axis=3, concat_axis=0, tiled=True)]
  transfers between devices with their start and end apart: 8 -> 8, of which waited for: 6 -> 6; matrix products, arithmetic and copies ran while one was open for 4% -> 5% of each run, Pallas kernels for 0% -> 0%
where the time goes in v1:
time: 512 us; the launch traced here: 511 us
  waiting for transfers between devices  274 us (54%)
  blocking collectives  86.7 us (17%)
  local copies, waits for them, and re-layouts  48.3 us (9%)
  matrix products  39.2 us (8%)
  other arithmetic  38.9 us (8%)
  between operations  15.2 us (3%)
  starting transfers between devices  7.66 us (1%)
    ppermute x1, waiting for transfers between devices, shifted(): return lax.ppermute(x, axis, pairs)  89.7 us
    reduce_scatter x1, waiting for transfers between devices, on_device(): lax.psum_scatter(product.reshape(row_count * lax.axis_size('tile'), frame...  74.2 us
    unnamed x3, blocking collectives  57.1 us
    reduce_scatter x1, waiting for transfers between devices, on_device(): lax.psum_scatter(product.reshape(lax.axis_size('tile') * row_count, frame...  49.1 us
    reduce_scatter x1, waiting for transfers between devices, on_device(): lax.psum_scatter(local_kv, 'tile', scatter_dimension=0, tiled=True)  28.2 us
    all_gather x1, waiting for transfers between devices, on_device(): portion = lax.all_gather(hidden, 'tile', axis=0, tiled=True)  25.9 us
    all_to_all x1, blocking collectives, _refer_shards(): lax.all_to_all(jnp.stack(jnp.split(block_here, lax.axis_size(axis_id), ax...  19.9 us
    dot_general x1, matrix products, on_device(): jnp.dot(portion.reshape(-1, model_width), w_flat, preferred_element_type=...  16 us
  transfers between devices with their start and end apart: 8, of which 6 were waited for; matrix products, arithmetic and copies ran while one was open for 5% of the time, Pallas kernels for 0%

profile of v1, /device:TPU:0, one launch (start us, length us, event | category | flops | bytes accessed | tf_op | source)
XLA Modules:
  0.0 510.6 jit_solution(3814639003826604296)
XLA Ops:
  9.1 4.0 reshape.56
  13.1 4.0 reshape.57
  20.7 28.2 %reduce-scatter.4.cloned.1.call-done = f32[560,112]{1,0:T(8,128)} async-done(((f32[2240,112]{1,0:T(8,128)}), f32[560,112]{1,0:T(8,128)}) %reduce-scatter.4.cloned.1.call-update) | async-done | bytes 250896 | tf_op jit(solution)/shard_map/reduce_scatter | solution.py:88
  50.4 7.2 %collective-permute-done = f32[560,112]{1,0:T(8,128)S(1)} collective-permute-done((f32[560,112]{1,0:T(8,128)}, f32[560,112]{1,0:T(8,128)S(1)}, u32[]{:S(2)}, u32[]{:S(2)}) %collective-permute-start) | collective-permute-done | bytes 250912 | tf_op jit(solution)/shard_map/ppermute | solution.py:26
  62.0 10.2 %all-reduce.3 = f32[2240]{0:T(1024)S(1)} all-reduce(f32[2240]{0:T(1024)S(1)} %convert_reduce_fusion), channel_id=5, replica_groups=mesh['blk'=8,'tile'=4] {'tile'}, use_global_device_ids=true, to_apply=%region_2.3.clone | all-reduce | flops 2240 | bytes 17920
  79.2 4.3 reshape.60
  87.0 36.8 %all-reduce.1 = f32[4480]{0:T(1024)S(1)} all-reduce(f32[4480]{0:T(1024)S(1)} %multiply_dynamic-update-slice_fusion), channel_id=3, replica_groups=mesh['blk'=8,'tile'=4] {'blk'}, use_global_device_ids=true, to_apply=%add.1 | all-reduce | flops 4480 | bytes 35840
  123.9 8.9 %while.16 = (s32[]{:T(128)}, f32[560,112]{1,0:T(8,128)S(1)}, f32[560]{0:T(1024)S(1)}, s32[]{:T(128)}, f32[8,560,112]{2,1,0:T(8,128)}, /*index=5*/f32[8,560]{1,0:T(8,128)S(1)}, s32[]{:T(128)}, s32[]{:T(128)}) while((s32[]{:T(128)}, f32[560,112]{1,0:T(8,128)S(1)}, f32[560]{0:T(1024)S(1)}, s32[]{:T(128)}, f32[8,560,112]{2,1,0:T(8,128)}, ...), condition=%wide.region_4.5_spmd.clone, body=%wide.region_3.4_spmd.clone.sunk | while | flops 189844 | bytes 763955 | solution.py:41
  133.0 10.1 %all-reduce.2 = f32[2240]{0:T(1024)S(1)} all-reduce(f32[2240]{0:T(1024)S(1)} %add_dynamic-update-slice_fusion), channel_id=1, replica_groups=mesh['blk'=8,'tile'=4] {'tile'}, use_global_device_ids=true, to_apply=%add.2 | all-reduce | flops 2240 | bytes 17920
  146.3 9.6 %all_gather.25 = f32[2240,112]{1,0:T(8,128)S(1)} all-gather(f32[560,112]{1,0:T(8,128)S(1)} %multiply_add_fusion.1), channel_id=1, replica_groups=mesh['blk'=8,'tile'=4] {'tile'}, dimensions={0}, use_global_device_ids=true | all-gather | bytes 1254400 | tf_op jit(solution)/shard_map/all_gather | solution.py:93
  161.9 3.7 reshape.62
  167.6 19.9 %all_to_all.5 = bf16[4,8,2,16,560]{4,3,2,1,0:T(8,128)(2,1)S(1)} all-to-all(bf16[4,8,2,16,560]{4,3,2,1,0:T(8,128)(2,1)S(1)} %pad_maximum_fusion.1), channel_id=1, replica_groups=mesh['blk'=8,'tile'=4] {'tile'}, dimensions={0} | all-to-all | bytes 2293760 | tf_op jit(solution)/shard_map/all_to_all | solution.py:13
  187.6 6.2 %fusion.3 = f32[32,2,16,2240]{3,2,1,0:T(8,128)} fusion(bf16[32,2,16,560]{3,2,1,0:T(8,128)(2,1)S(1)} %bitcast.94, bf16[560,2240]{1,0:T(8,128)(2,1)S(1)} %copy-done), kind=kOutput, calls=%fused_computation.21 | convolution fusion | flops 2569011200 | bytes 12830720 | tf_op jit(solution)/shard_map/dot_general | solution.py:105
  193.9 74.2 %reduce-scatter.6.cloned.1.call-done = f32[8,2,16,2240]{3,2,1,0:T(8,128)} async-done(((f32[32,2,16,2240]{3,2,1,0:T(8,128)}), f32[8,2,16,2240]{3,2,1,0:T(8,128)}) %reduce-scatter.6.cloned.1.call-update) | async-done | bytes 2293776 | tf_op jit(solution)/shard_map/reduce_scatter | solution.py:108
  271.3 11.4 %copy.35 = bf16[280,8,2,1024]{3,1,2,0:T(8,128)(2,1)} copy(bf16[280,8,2,1024]{3,2,1,0:T(2,128)(2,1)} %bitcast.91) | data formatting | bytes 18350080
  282.7 25.9 %all-gather.5.cloned.1.call-done = bf16[32,2,16,2240]{3,2,1,0:T(8,128)(2,1)} async-done(((bf16[8,2,16,2240]{3,2,1,0:T(8,128)(2,1)}), bf16[32,2,16,2240]{3,2,1,0:T(8,128)(2,1)}) %all-gather.5.cloned.1.call-update) | async-done | bytes 4587536 | tf_op jit(solution)/shard_map/all_gather | solution.py:117
  308.6 16.0 %multiply_convert_fusion = bf16[1024,2048]{1,0:T(8,128)(2,1)} fusion(bf16[1024,2240]{1,0:T(8,128)(2,1)} %bitcast.97, bf16[2240,2048]{1,0:T(8,128)(2,1)} %bitcast.92), kind=kOutput, calls=%fused_computation.13 | convolution fusion | flops 9405726720 | bytes 17956864 | tf_op jit(solution)/shard_map/dot_general | solution.py:118
  324.6 7.8 %reshape.65 = bf16[32,2,16,2,1024]{4,3,2,1,0:T(2,128)(2,1)} reshape(bf16[1024,2048]{1,0:T(8,128)(2,1)} %multiply_convert_fusion) | data formatting | bytes 8388608 | tf_op jit(solution)/shard_map/reshape | solution.py:120
  332.4 3.5 copy.28
  335.9 12.0 %add_convert_fusion = bf16[32,2,16,2,1024]{4,2,1,0,3:T(8,128)(2,1)S(1)} fusion(bf16[32,2,16,2,1024]{4,2,1,0,3:T(8,128)(2,1)S(1)} %copy.28, f32[2,1024]{1,0:T(2,128)S(1)} %get-tuple-element.161, f32[2,1024]{1,0:T(2,128)S(1)} %get-tuple-element.162, f32[2,1024]{1,0:T(2,128)S(1)} %get-tuple-element.155, f32[2,1024]{1,0:T(2,128)S(1)} %get-tuple-element.156, ...), kind=kLoop, calls=%fused_computation.12 | loop fusion | flops 56623104 | bytes 8462336 | tf_op jit(solution)/shard_map/convert_element_type | solution.py:121
  347.9 3.9 collective-permute-start.2
  351.9 89.7 %collective-permute-done.2 = bf16[32,2,16,2,1024]{4,2,1,0,3:T(8,128)(2,1)S(1)} collective-permute-done((bf16[32,2,16,2,1024]{4,2,1,0,3:T(8,128)(2,1)S(1)}, bf16[32,2,16,2,1024]{4,2,1,0,3:T(8,128)(2,1)S(1)}, u32[]{:S(2)}, u32[]{:S(2)}) %collective-permute-start.2) | collective-permute-done | bytes 4194336 | tf_op jit(solution)/shard_map/ppermute | solution.py:47
  444.7 7.2 %convolution_convert_fusion = bf16[32,2,16,2240]{3,2,1,0:T(8,128)(2,1)} fusion(bf16[1024,2240]{0,1:T(8,128)(2,1)S(1)} %bitcast.99, f32[32,2,16,2,1024]{4,2,1,0,3:T(8,128)S(1)} %multiply_add_fusion), kind=kOutput, calls=%fused_computation.14 | convolution fusion | flops 4706205696 | bytes 17563648 | tf_op jit(solution)/shard_map/dot_general | solution.py:132
  452.0 49.1 %reduce-scatter.8.cloned.1.call-done = bf16[8,2,16,2240]{3,2,1,0:T(8,128)(2,1)} async-done(((bf16[32,2,16,2240]{3,2,1,0:T(8,128)(2,1)}), bf16[8,2,16,2240]{3,2,1,0:T(8,128)(2,1)}) %reduce-scatter.8.cloned.1.call-update) | async-done | bytes 1146896 | tf_op jit(solution)/shard_map/reduce_scatter | solution.py:133
  (90 shorter events, 50.0 us)
Async XLA Ops:
  6.5 181.0 %copy-start = (bf16[560,2240]{1,0:T(8,128)(2,1)S(1)}, bf16[560,2240]{1,0:T(8,128)(2,1)}, u32[]{:S(2)}) copy-start(bf16[560,2240]{1,0:T(8,128)(2,1)} %param.15) | copy-start | bytes 7526404
  6.5 42.4 %reduce-scatter.4.cloned.1.call-start = ((), (), s32[]{:S(2)}) async-start(), calls=%async_computation.4 | async-start | bytes 1433600 | tf_op jit(solution)/shard_map/reduce_scatter | solution.py:88
  13.1 46.2 %copy-start.7 = (u32[32]{0:T(128)S(1)}, u32[32]{0:T(128)}, u32[]{:S(2)}) copy-start(u32[32]{0:T(128)} %constant.77) | copy-start | bytes 388
  20.6 56.6 %copy-start.8 = (u32[32]{0:T(128)S(1)}, u32[32]{0:T(128)}, u32[]{:S(2)}) copy-start(u32[32]{0:T(128)} %constant.72) | copy-start | bytes 388
  20.6 103.3 %all-gather.7.cloned.1.call-start = ((), (), s32[]{:S(2)}) async-start(), calls=%async_computation.8 | async-start | bytes 2580480 | tf_op jit(solution)/shard_map/all_gather | solution.py:31
  48.9 8.6 %collective-permute-start = (f32[560,112]{1,0:T(8,128)}, f32[560,112]{1,0:T(8,128)S(1)}, u32[]{:S(2)}, u32[]{:S(2)}) collective-permute-start(f32[560,112]{1,0:T(8,128)} %reduce-scatter.4.cloned.1.call-done), channel_id=1, source_target_pairs={{0,4},{4,0},{8,12},{12,8},{16,20},{20,16},{24,28},{28,24},{1,5},{5... | collective-permute-start | bytes 752648 | tf_op jit(solution)/shard_map/ppermute | solution.py:26
  59.3 208.8 %reduce-scatter.6.cloned.1.call-start = ((), (), s32[]{:S(2)}) async-start(), calls=%async_computation.5 | async-start | bytes 11796480 | tf_op jit(solution)/shard_map/reduce_scatter | solution.py:108
  72.3 14.5 %collective-permute-start.1 = (f32[560]{0:T(1024)S(1)}, f32[560]{0:T(1024)S(1)}, u32[]{:S(2)}, u32[]{:S(2)}) collective-permute-start(f32[560]{0:T(1024)S(1)} %dynamic-slice.3), channel_id=1, source_target_pairs={{0,4},{4,0},{8,12},{12,8},{16,20},{20,16},{24,28},{28,24},{1,5},{5... | collective-permute-start | bytes 6728 | tf_op jit(solution)/shard_map/ppermute | solution.py:26
  86.8 59.4 %copy-start.4 = (f32[560,112]{1,0:T(8,128)S(1)}, f32[560,112]{1,0:T(8,128)}, u32[]{:S(2)}) copy-start(f32[560,112]{1,0:T(8,128)} %reduce-scatter.4.cloned.1.call-done) | copy-start | bytes 752644
  143.2 12.7 %copy-start.2 = (f32[256,20,112]{0,2,1:T(8,128)S(1)}, f32[256,20,112]{0,2,1:T(8,128)}, u32[]{:S(2)}) copy-start(f32[256,20,112]{0,2,1:T(8,128)} %copy.26) | copy-start | bytes 6881284
  193.8 74.3 %copy-start.3 = (bf16[8,2,16,2240]{3,2,1,0:T(8,128)(2,1)S(1)}, bf16[8,2,16,2240]{3,2,1,0:T(8,128)(2,1)}, u32[]{:S(2)}) copy-start(bf16[8,2,16,2240]{3,2,1,0:T(8,128)(2,1)} %param.11) | copy-start | bytes 3440644
  193.8 114.8 %all-gather.5.cloned.1.call-start = ((), (), s32[]{:S(2)}) async-start(), calls=%async_computation.6 | async-start | bytes 5898240 | tf_op jit(solution)/shard_map/all_gather | solution.py:117
  271.0 230.2 %reduce-scatter.8.cloned.1.call-start = ((), (), s32[]{:S(2)}) async-start(), calls=%async_computation.7 | async-start | bytes 5898240 | tf_op jit(solution)/shard_map/reduce_scatter | solution.py:133
  271.2 11.4 %copy-start.5 = (f32[3,3,2,1024]{3,2,1,0:T(2,128)S(1)}, f32[3,3,2,1024]{3,2,1,0:T(2,128)}, u32[]{:S(2)}) copy-start(f32[3,3,2,1024]{3,2,1,0:T(2,128)} %param.18) | copy-start | bytes 221188
  335.9 15.9 %copy-start.6 = (f32[3,2,1024]{2,1,0:T(2,128)S(1)}, f32[3,2,1024]{2,1,0:T(2,128)}, u32[]{:S(2)}) copy-start(f32[3,2,1024]{2,1,0:T(2,128)} %param.19) | copy-start | bytes 73732
  335.9 108.8 %slice-start = ((s8[4587520]{0:T(1024)(128)(4,1)}), s8[4194304]{0:T(1024)(128)(4,1)S(1)}, s32[]{:S(2)}) async-start(s8[4587520]{0:T(1024)(128)(4,1)} %bitcast.98), calls=%async_computation.9 | async-start | bytes 8388608
  347.9 93.6 %collective-permute-start.2 = (bf16[32,2,16,2,1024]{4,2,1,0,3:T(8,128)(2,1)S(1)}, bf16[32,2,16,2,1024]{4,2,1,0,3:T(8,128)(2,1)S(1)}, u32[]{:S(2)}, u32[]{:S(2)}) collective-permute-start(bf16[32,2,16,2,1024]{4,2,1,0,3:T(8,128)(2,1)S(1)} %add_convert_fusion), channel_id=1, source_target_pairs={{0,4},{4,8},{8,12},{12,16},{16,20},{20,24},{24,28},{1,5},{5,9},{9,... | collective-permute-start | bytes 12582920 | tf_op jit(solution)/shard_map/ppermute | solution.py:47
  441.5 3.2 slice-start.1
  444.7 59.3 %copy-start.1 = (bf16[560,2240]{1,0:T(8,128)(2,1)S(1)}, bf16[560,2240]{1,0:T(8,128)(2,1)}, u32[]{:S(2)}) copy-start(bf16[560,2240]{1,0:T(8,128)(2,1)} %param.15) | copy-start | bytes 7526404
Sparse Core Ops, SparseCore 0:
  20.7 28.1 reduce-scatter.3
  59.4 51.7 all-gather.6
  193.9 74.0 reduce-scatter.5
  271.1 37.4 all-gather.4
  452.1 48.9 reduce-scatter.7
